TPU v7x, 128 devices: a whole 4x4x4 slice. The times are simulated.
128 devices in a mesh: group: 4 (over x), bulk: 32 (over z, y, core).
Axes of the slice: x: 4, y: 4, z: 4, core: 2. Of those that a mesh axis runs over, the one named last changes fastest.
Arguments:
- rhs: float32 [512, 64, 128], P(('group', 'bulk')), may hold values from -90 to 90, as said below
- diag_tiles: float32 [512, 128, 128], P(('group', 'bulk')), may hold values from -0.06 to 0.06
- offdiag_blocks: float32 [512, 11, 128, 128], P(('group', 'bulk')), may hold values from -0.026 to 0.026
- coupling: float32 [256, 4, 128, 128], P(('group', 'bulk')), may hold values from -0.05 to 0.05, as said below
- col_index: int32 [512, 11], replicated, may hold values from 0 to 511, as said below
- load: int32 [512], replicated, may hold values from 3 to 11
- new_slot: int32 [512], replicated, may hold values from 0 to 511, as said below
Outputs:
- solution_out: float32 [512, 64, 128], P(('group', 'bulk'))
- residual_out: float32 [512, 64, 128], P(('group', 'bulk'))
Inputs may be any that keep to these rules, and one draw needn't show every extreme that they name: `rhs`: made of random entries times scales of the rows and of the columns. `coupling`: entry [d * 2 + k, h] is the transpose of entry [(h * 32 + d % 32) * 2 + k, d // 32]. `col_index`: for each part g and each tile position t, the column t of the 128 block rows of part g is a permutation of that part's slots g * 128 to (g + 1) * 128 - 1. Of the 44 entries of the 4 block rows of one device (slots d * 4 to (d + 1) * 4 - 1), at most 2 name slots of any one device, and exactly 2 name slots of some device. `new_slot`: A permutation. On every device exactly one block row moves, from a slot k with 2 <= k % 4; it stays in its part, goes from owner b to owner b XOR m, where m (1 to 31) is one number for the whole part, and takes the slot that the moving row of that device leaves.
All inputs are finite; a program needn't handle non-finite values.
Results may differ from a plain program's by a relative error of at most 0.0003.
Values sent between devices are 32-bit elements; how exact they have to be, the bound alone decides.
A program may use at most 64 MiB of HBM per device.

v0:
```python
import jax
import jax.numpy as jnp
from jax import lax
from jax.sharding import PartitionSpec as P

highest = lax.Precision.HIGHEST
diagonal_shift = 4.0


def chol_apply(matrix, right):
    factor = jnp.linalg.cholesky(matrix)
    middle = lax.linalg.triangular_solve(factor, right, left_side=True, lower=True)
    return lax.linalg.triangular_solve(factor, middle, left_side=True, lower=True, transpose_a=True)


def gram(left, right):
    return jnp.einsum("snt,smt->nm", left, right, precision=highest)


def sym(m):
    return 0.5 * (m + m.T)


def mm(a, b):
    return jnp.dot(a, b, precision=highest)


def off_part(vectors, diag, masked, column_ids, coupling):
    boundary_rows = coupling.shape[0]
    part_count = coupling.shape[1]
    border = lax.all_gather(vectors[:boundary_rows], "group", axis=0, tiled=True)
    own = jnp.einsum("rnj,rij->rni", vectors, diag, precision=highest)
    returned = jnp.einsum("rni,rkij->rknj", vectors, masked, precision=highest)
    panel = lax.all_gather(vectors, "bulk", axis=0, tiled=True)
    picked = panel[column_ids]
    own = own + jnp.einsum("rknj,rkij->rni", picked, masked, precision=highest)
    border = border.reshape((part_count, boundary_rows) + vectors.shape[1:])
    crossed = jnp.einsum("khij,hknj->kni", coupling, border, precision=highest)
    return (own.at[:boundary_rows].add(crossed), returned.reshape((-1,) + vectors.shape[1:]), panel)


def coefficients(n0, n1, n2, n3):
    n = n0.shape[0]
    eye = jnp.eye(n, dtype=n0.dtype)
    n0, n1, n2, n3 = (sym(n0), sym(n1), sym(n2), sym(n3))
    delta = chol_apply(diagonal_shift * n0 + n1, n1)
    alpha = (eye - delta) / diagonal_shift
    b = -alpha
    cross = mm(delta.T, mm(n1, b))
    gram_new = sym(mm(delta.T, mm(n0, delta)) + cross + cross.T + mm(b.T, mm(n2, b)))
    beta = chol_apply(n0, gram_new)
    a = delta + beta
    c1 = mm(a.T, mm(n1, b))
    c2 = mm(a.T, mm(n2, b))
    pp = mm(a.T, mm(n0, a)) + c1 + c1.T + mm(b.T, mm(n2, b))
    pep = mm(a.T, mm(n1, a)) + c2 + c2.T + mm(b.T, mm(n3, b))
    alpha2 = chol_apply(sym(diagonal_shift * pp + pep), gram_new)
    ba = mm(b, alpha2)
    aa = mm(a, alpha2)
    sol = (alpha + aa, ba)
    res = (delta - diagonal_shift * aa, b - diagonal_shift * ba - aa, -ba)
    return (sol, res)


def local(rhs, diag_tiles, offdiag_blocks, coupling, col_index, load, new_slot):
    row_count = rhs.shape[0]
    off_count = offdiag_blocks.shape[1]
    bulk_count = lax.axis_size("bulk")
    group_rows = row_count * bulk_count
    group_base = lax.axis_index("group") * group_rows
    first = lax.axis_index("bulk") * row_count
    cols = lax.dynamic_slice_in_dim(col_index, group_base, group_rows) - group_base
    moved = lax.dynamic_slice_in_dim(new_slot, group_base, group_rows) - group_base
    loads = lax.dynamic_slice_in_dim(load, group_base + first, row_count)
    my_cols = lax.dynamic_slice_in_dim(cols, first, row_count)
    my_new = lax.dynamic_slice_in_dim(moved, first, row_count)
    tile_ids = jnp.arange(off_count, dtype=jnp.int32)
    mask = (tile_ids[None, :] < loads[:, None]).astype(jnp.float32)
    masked = offdiag_blocks * mask[:, :, None, None]
    u0 = rhs
    own, returned, panel0 = off_part(u0, diag_tiles, masked, my_cols, coupling)
    buffer = jax.ops.segment_sum(returned, my_cols.reshape(-1), num_segments=group_rows)
    u1 = own + lax.psum_scatter(buffer, "bulk", scatter_dimension=0, tiled=True)
    own, returned, panel1 = off_part(u1, diag_tiles, masked, my_cols, coupling)
    ids = jnp.concatenate([moved[my_cols.reshape(-1)], my_new])
    buffer = jax.ops.segment_sum(jnp.concatenate([returned, own]), ids, num_segments=group_rows)
    u2 = lax.psum_scatter(buffer, "bulk", scatter_dimension=0, tiled=True)
    inverse = jnp.zeros_like(moved).at[moved].set(jnp.arange(group_rows, dtype=jnp.int32))
    mine = lax.dynamic_slice_in_dim(inverse, first, row_count)
    v0, v1 = (panel0[mine], panel1[mine])
    grams = jnp.stack([gram(v0, v0), gram(v0, v1), gram(v1, v1), gram(v1, u2)])
    grams = lax.psum(grams, ("group", "bulk"))
    sol, res = coefficients(grams[0], grams[1], grams[2], grams[3])
    basis = jnp.concatenate([v0, v1, u2], axis=1)
    zero = jnp.zeros_like(sol[0])
    weights = jnp.concatenate(
        [jnp.concatenate(sol + (zero,), axis=0), jnp.concatenate(res, axis=0)], axis=1
    )
    out = jnp.einsum("mn,smt->snt", weights, basis, precision=highest)
    n = rhs.shape[1]
    return (out[:, :n], out[:, n:])


def solution(mesh):
    return jax.shard_map(
        local,
        mesh=mesh,
        in_specs=(
            P(("group", "bulk"), None, None),
            P(("group", "bulk"), None, None),
            P(("group", "bulk"), None, None, None),
            P(("group", "bulk"), None, None, None),
            P(),
            P(),
            P(),
        ),
        out_specs=(P(("group", "bulk"), None, None), P(("group", "bulk"), None, None)),
        check_vma=False,
    )
```

profile of v0, /device:TPU:1, one launch (start us, length us, event | category | flops | bytes accessed | tf_op | source)
XLA Modules:
  0.0 494.6 jit_solution(10182201475086260046)
XLA Ops:
  9.8 3.8 fusion.4
  16.0 6.9 %scatter_fusion = f32[128,64,128]{2,1,0:T(8,128)} fusion(f32[128,64,128]{2,1,0:T(8,128)} %broadcast.140.clone, s32[44]{0:T(128)S(1)} %reshape.206, f32[44,64,128]{2,1,0:T(8,128)S(1)} %bitcast.248), kind=kCustom, calls=%fused_computation.6 | custom fusion | flops 360448 | bytes 4325552 | tf_op jit(solution)/shard_map/scatter-add | solution.py:82
  25.9 12.7 %all_gather.13 = f32[8,64,128]{2,1,0:T(8,128)} all-gather(f32[2,64,128]{2,1,0:T(8,128)} %slice.81), channel_id=1, replica_groups=mesh['group'=4,'bulk'=32] {'group'}, dimensions={0}, use_global_device_ids=true | all-gather | bytes 327680 | tf_op jit(solution)/shard_map/all_gather | solution.py:31
  38.5 21.5 %all-gather.3.cloned.1.call-done = f32[128,64,128]{2,1,0:T(8,128)} async-done(((f32[4,64,128]{2,1,0:T(8,128)}), f32[128,64,128]{2,1,0:T(8,128)}) %all-gather.3.cloned.1.call-update) | async-done | bytes 4194320 | tf_op jit(solution)/shard_map/all_gather | solution.py:34
  60.1 4.0 gather_fusion.1
  64.1 4.8 fusion.12
  72.4 71.0 %reduce-scatter.3.cloned.1.call-done = f32[4,64,128]{2,1,0:T(8,128)} async-done(((f32[128,64,128]{2,1,0:T(8,128)}), f32[4,64,128]{2,1,0:T(8,128)}) %reduce-scatter.3.cloned.1.call-update) | async-done | bytes 131088 | tf_op jit(solution)/shard_map/reduce_scatter | solution.py:83
  147.7 10.6 %all_gather.15 = f32[8,64,128]{2,1,0:T(8,128)} all-gather(f32[2,64,128]{2,1,0:T(8,128)S(1)} %slice.102), channel_id=1, replica_groups=mesh['group'=4,'bulk'=32] {'group'}, dimensions={0}, use_global_device_ids=true | all-gather | bytes 327680 | tf_op jit(solution)/shard_map/all_gather | solution.py:31
  158.3 4.1 fusion.2
  162.4 31.4 %all-gather.5.cloned.1.call-done = f32[128,64,128]{2,1,0:T(8,128)} async-done(((f32[4,64,128]{2,1,0:T(8,128)}), f32[128,64,128]{2,1,0:T(8,128)}) %all-gather.5.cloned.1.call-update) | async-done | bytes 4194320 | tf_op jit(solution)/shard_map/all_gather | solution.py:34
  193.8 3.9 gather_fusion.4
  197.7 4.9 fusion.15
  204.1 2.5 broadcast.140
  206.6 6.9 %scatter_fusion.1 = f32[128,64,128]{2,1,0:T(8,128)} fusion(f32[128,64,128]{2,1,0:T(8,128)} %broadcast.140, s32[48]{0:T(128)S(1)} %pad_add_fusion, f32[48,64,128]{2,1,0:T(8,128)S(1)} %pad_maximum_fusion), kind=kCustom, calls=%fused_computation.7 | custom fusion | flops 393216 | bytes 4718784 | tf_op jit(solution)/shard_map/scatter-add | solution.py:86
  214.9 2.7 gather_fusion
  217.9 2.7 gather_fusion.2
  221.1 72.2 %reduce-scatter.5.cloned.1.call-done = f32[4,64,128]{2,1,0:T(8,128)} async-done(((f32[128,64,128]{2,1,0:T(8,128)}), f32[4,64,128]{2,1,0:T(8,128)}) %reduce-scatter.5.cloned.1.call-update) | async-done | bytes 131088 | tf_op jit(solution)/shard_map/reduce_scatter | solution.py:87
  295.2 146.3 %all-reduce.2.cloned.1.call-done = f32[4,64,64]{2,1,0:T(8,128)} async-done(((f32[4,64,64]{2,1,0:T(8,128)}), f32[4,64,64]{2,1,0:T(8,128)}) %all-reduce.2.cloned.1.call-update) | async-done | bytes 65552 | tf_op jit(solution)/shard_map/psum | solution.py:92
  443.6 5.9 %cholesky.59 = f32[64,64]{1,0:T(8,128)S(1)} custom-call(f32[64,64]{1,0:T(8,128)S(1)} %copy.82), custom_call_target="Cholesky" | custom-call | tf_op jit(solution)/shard_map/jit(cholesky)/cholesky | solution.py:11
  450.8 4.9 custom-call.13
  456.7 5.9 %cholesky.70 = f32[64,64]{1,0:T(8,128)S(1)} custom-call(f32[64,64]{1,0:T(8,128)S(1)} %copy.85), custom_call_target="Cholesky" | custom-call | tf_op jit(solution)/shard_map/jit(cholesky)/cholesky | solution.py:11
  463.9 4.9 custom-call.15
  473.9 5.8 %cholesky.81 = f32[64,64]{1,0:T(8,128)S(1)} custom-call(f32[64,64]{1,0:T(8,128)S(1)} %fusion.51), custom_call_target="Cholesky" | custom-call | tf_op jit(solution)/shard_map/jit(cholesky)/cholesky | solution.py:11
  481.1 4.9 custom-call.17
  (120 shorter events, 35.1 us)
Async XLA Ops:
  7.2 63.1 %copy-start = (f32[2,4,128,128]{3,2,1,0:T(8,128)S(1)}, f32[2,4,128,128]{3,2,1,0:T(8,128)}, u32[]{:S(2)}) copy-start(f32[2,4,128,128]{3,2,1,0:T(8,128)} %param.19) | copy-start | bytes 1572868
  7.2 52.9 %all-gather.3.cloned.1.call-start = ((), (), s32[]{:S(2)}) async-start(), calls=%async_computation.2 | async-start | bytes 4325376 | tf_op jit(solution)/shard_map/all_gather | solution.py:34
  7.9 135.5 %reduce-scatter.3.cloned.1.call-start = ((), (), s32[]{:S(2)}) async-start(), calls=%async_computation.3 | async-start | bytes 4325376 | tf_op jit(solution)/shard_map/reduce_scatter | solution.py:83
  22.9 0.9 copy-start.4
  22.9 41.2 %copy-start.1 = (f32[4,11,128,128]{3,2,1,0:T(8,128)S(1)}, f32[4,11,128,128]{3,2,1,0:T(8,128)}, u32[]{:S(2)}) copy-start(f32[4,11,128,128]{3,2,1,0:T(8,128)} %param.18) | copy-start | bytes 8650756
  22.9 170.9 %all-gather.5.cloned.1.call-start = ((), (), s32[]{:S(2)}) async-start(), calls=%async_computation.4 | async-start | bytes 4325376 | tf_op jit(solution)/shard_map/all_gather | solution.py:34
  64.1 4.8 copy-start.7
  64.1 6.1 %copy-start.6 = (f32[8,64,128]{2,1,0:T(8,128)S(1)}, f32[8,64,128]{2,1,0:T(8,128)}, u32[]{:S(2)}) copy-start(f32[8,64,128]{2,1,0:T(8,128)} %all_gather.13) | copy-start | bytes 786436
  145.0 148.3 %reduce-scatter.5.cloned.1.call-start = ((), (), s32[]{:S(2)}) async-start(), calls=%async_computation.5 | async-start | bytes 4325376 | tf_op jit(solution)/shard_map/reduce_scatter | solution.py:87
  197.7 4.9 copy-start.3
  197.7 4.9 %copy-start.8 = (f32[4,128,128]{2,1,0:T(8,128)S(1)}, f32[4,128,128]{2,1,0:T(8,128)}, u32[]{:S(2)}) copy-start(f32[4,128,128]{2,1,0:T(8,128)} %param.17) | copy-start | bytes 786436
  197.7 5.6 %copy-start.5 = (f32[8,64,128]{2,1,0:T(8,128)S(1)}, f32[8,64,128]{2,1,0:T(8,128)}, u32[]{:S(2)}) copy-start(f32[8,64,128]{2,1,0:T(8,128)} %all_gather.15) | copy-start | bytes 786436
  197.7 6.2 %copy-start.2 = (f32[4,11,128,64]{2,3,1,0:T(8,128)S(1)}, f32[4,11,128,64]{2,3,1,0:T(8,128)}, u32[]{:S(2)}) copy-start(f32[4,11,128,64]{2,3,1,0:T(8,128)} %fusion.2) | copy-start | bytes 4325380
  213.5 228.1 %all-reduce.2.cloned.1.call-start = ((), (), s32[]{:S(2)}) async-start(), calls=%async_computation.6 | async-start | bytes 262144 | tf_op jit(solution)/shard_map/psum | solution.py:92
  294.5 192.4 %copy-start.9 = (f32[4,64,128]{2,1,0:T(8,128)S(1)}, f32[4,64,128]{2,1,0:T(8,128)}, u32[]{:S(2)}) copy-start(f32[4,64,128]{2,1,0:T(8,128)} %reduce-scatter.5.cloned.1.call-done) | copy-start | bytes 393220
Sparse Core Ops, SparseCore 0:
  10.2 49.7 all-gather.2
  63.7 79.6 reduce-scatter.2
  146.2 47.5 all-gather.4
  213.6 79.7 reduce-scatter.4
  298.5 142.9 all-reduce.1
where the time goes:
time: 496 us; the launch traced here: 495 us
  waiting for transfers between devices  343 us (69%)
  other arithmetic  55.1 us (11%)
  matrix products  30.5 us (6%)
  local copies, waits for them, and re-layouts  28.1 us (6%)
  blocking collectives  23.2 us (5%)
  between operations  14.3 us (3%)
    psum x1, waiting for transfers between devices, local(): grams = lax.psum(grams, ('group', 'bulk'))  146 us
    reduce_scatter x1, waiting for transfers between devices, local(): u2 = lax.psum_scatter(buffer, 'bulk', scatter_dimension=0, tiled=True)  72.2 us
    reduce_scatter x1, waiting for transfers between devices, local(): u1 = own + lax.psum_scatter(buffer, 'bulk', scatter_dimension=0, tiled=True)  71 us
    all_gather x2, waiting for transfers between devices, off_part(): panel = lax.all_gather(vectors, 'bulk', axis=0, tiled=True)  52.9 us
    all_gather x2, blocking collectives, off_part(): lax.all_gather(vectors[:boundary_rows], 'group', axis=0, tiled=True)  23.2 us
    another operation x9, other arithmetic, chol_apply(): factor = jnp.linalg.cholesky(matrix)  19.6 us
    another operation x6, other arithmetic, chol_apply(): lax.linalg.triangular_solve(factor, middle, left_side=True, lower=True, t...  16.6 us
  transfers between devices with their start and end apart: 5, of which 5 were waited for; matrix products, arithmetic and copies ran while one was open for 9% of the time, Pallas kernels for 0%

commit v1 on v0

--- a/solution.py
+++ b/solution.py
@@ -5,6 +5,11 @@
 
 highest = lax.Precision.HIGHEST
 diagonal_shift = 4.0
+
+
+def gather_from_all(array, axis, dim):
+    copies = jnp.concatenate([array] * lax.axis_size(axis), axis=dim)
+    return lax.all_to_all(copies, axis, dim, dim, tiled=True)
 
 
 def chol_apply(matrix, right):
@@ -31,7 +36,7 @@
     border = lax.all_gather(vectors[:boundary_rows], "group", axis=0, tiled=True)
     own = jnp.einsum("rnj,rij->rni", vectors, diag, precision=highest)
     returned = jnp.einsum("rni,rkij->rknj", vectors, masked, precision=highest)
-    panel = lax.all_gather(vectors, "bulk", axis=0, tiled=True)
+    panel = gather_from_all(vectors, "bulk", 0)
     picked = panel[column_ids]
     own = own + jnp.einsum("rknj,rkij->rni", picked, masked, precision=highest)
     border = border.reshape((part_count, boundary_rows) + vectors.shape[1:])

time: 496 us -> 514 us (1.036)
  waiting for transfers between devices: 343 us -> 302 us
  local copies, waits for them, and re-layouts: 28.1 us -> 68.2 us
  starting transfers between devices: 0.2 us -> 17.3 us
    all_to_all x0 -> x2, waiting for transfers between devices: none -> 75.2 us  [gather_from_all(): return lax.all_to_all(copies, axis, dim, dim, tiled=True)]
    reduce_scatter x1, waiting for transfers between devices: 71 us -> 8.16 us  [local(): u1 = own + lax.psum_scatter(buffer, 'bulk', scatter_dimension=0, tiled=True)]
    all_gather x2 -> x0, waiting for transfers between devices: 52.9 us -> none  [off_part(): panel = lax.all_gather(vectors, 'bulk', axis=0, tiled=True)]
    unnamed x21 -> x80, local copies, waits for them, and re-layouts: 0.95 us -> 40.2 us
    all_to_all x0 -> x2, starting transfers between devices: none -> 17.2 us  [gather_from_all(): return lax.all_to_all(copies, axis, dim, dim, tiled=True)]
  transfers between devices with their start and end apart: 5 -> 5, of which waited for: 5 -> 5; matrix products, arithmetic and copies ran while one was open for 9% -> 10% of each run, Pallas kernels for 0% -> 0%
where the time goes in v1:
time: 514 us; the launch traced here: 512 us
  waiting for transfers between devices  302 us (59%)
  local copies, waits for them, and re-layouts  68.2 us (13%)
  other arithmetic  57.7 us (11%)
  matrix products  29.7 us (6%)
  blocking collectives  22.8 us (4%)
  starting transfers between devices  17.3 us (3%)
  between operations  14.3 us (3%)
    psum x1, waiting for transfers between devices, local(): grams = lax.psum(grams, ('group', 'bulk'))  146 us
    all_to_all x2, waiting for transfers between devices, gather_from_all(): return lax.all_to_all(copies, axis, dim, dim, tiled=True)  75.2 us
    reduce_scatter x1, waiting for transfers between devices, local(): u2 = lax.psum_scatter(buffer, 'bulk', scatter_dimension=0, tiled=True)  72.6 us
    unnamed x80, local copies, waits for them, and re-layouts  40.2 us
    all_gather x2, blocking collectives, off_part(): lax.all_gather(vectors[:boundary_rows], 'group', axis=0, tiled=True)  22.8 us
    another operation x9, other arithmetic, chol_apply(): factor = jnp.linalg.cholesky(matrix)  19.6 us
    all_to_all x2, starting transfers between devices, gather_from_all(): return lax.all_to_all(copies, axis, dim, dim, tiled=True)  17.2 us
    another operation x6, other arithmetic, chol_apply(): lax.linalg.triangular_solve(factor, middle, left_side=True, lower=True, t...  16.6 us
  transfers between devices with their start and end apart: 5, of which 5 were waited for; matrix products, arithmetic and copies ran while one was open for 10% of the time, Pallas kernels for 0%

profile of v1, /device:TPU:1, one launch (start us, length us, event | category | flops | bytes accessed | tf_op | source)
XLA Modules:
  0.0 512.4 jit_solution(33475403279514044)
XLA Ops:
  9.1 3.8 fusion.4
  15.4 6.9 %scatter_fusion = f32[128,64,128]{2,1,0:T(8,128)} fusion(f32[128,64,128]{2,1,0:T(8,128)} %broadcast.140.clone, s32[44]{0:T(128)S(1)} %reshape.206, f32[44,64,128]{2,1,0:T(8,128)S(1)} %bitcast.248), kind=kCustom, calls=%fused_computation.6 | custom fusion | flops 360448 | bytes 4325552 | tf_op jit(solution)/shard_map/scatter-add | solution.py:87
  43.3 9.8 %all-to-all-start = ((f32[128,64,128]{2,1,0:T(8,128)}), f32[128,64,128]{2,1,0:T(8,128)}, u32[]{:S(2)}, u32[]{:S(2)}) async-start(f32[128,64,128]{2,1,0:T(8,128)} %constant_dynamic-update-slice_fusion), calls=%async_computation | async-start | bytes 8388608 | tf_op jit(solution)/shard_map/all_to_all | solution.py:12
  53.8 11.3 %all_gather.6 = f32[8,64,128]{2,1,0:T(8,128)} all-gather(f32[2,64,128]{2,1,0:T(8,128)S(1)} %slice-done), channel_id=1, replica_groups=mesh['group'=4,'bulk'=32] {'group'}, dimensions={0}, use_global_device_ids=true | all-gather | bytes 327680 | tf_op jit(solution)/shard_map/all_gather | solution.py:36
  66.0 44.3 %all-to-all-done = f32[128,64,128]{2,1,0:T(8,128)} async-done(((f32[128,64,128]{2,1,0:T(8,128)}), f32[128,64,128]{2,1,0:T(8,128)}, u32[]{:S(2)}, u32[]{:S(2)}) %all-to-all-start) | async-done | bytes 4194336 | tf_op jit(solution)/shard_map/all_to_all | solution.py:12
  110.3 3.9 gather_fusion.1
  114.2 4.8 fusion.12
  122.5 8.2 %reduce-scatter.3.cloned.1.call-done = f32[4,64,128]{2,1,0:T(8,128)} async-done(((f32[128,64,128]{2,1,0:T(8,128)}), f32[4,64,128]{2,1,0:T(8,128)}) %reduce-scatter.3.cloned.1.call-update) | async-done | bytes 131088 | tf_op jit(solution)/shard_map/reduce_scatter | solution.py:88
  152.7 7.4 %all-to-all-start.1 = ((f32[128,64,128]{2,1,0:T(8,128)}), f32[128,64,128]{2,1,0:T(8,128)}, u32[]{:S(2)}, u32[]{:S(2)}) async-start(f32[128,64,128]{2,1,0:T(8,128)} %constant_dynamic-update-slice_fusion.32), calls=%async_computation.2 | async-start | bytes 8388608 | tf_op jit(solution)/shard_map/all_to_all | solution.py:12
  165.3 11.5 %all_gather.7 = f32[8,64,128]{2,1,0:T(8,128)} all-gather(f32[2,64,128]{2,1,0:T(8,128)S(1)} %slice.102), channel_id=1, replica_groups=mesh['group'=4,'bulk'=32] {'group'}, dimensions={0}, use_global_device_ids=true | all-gather | bytes 327680 | tf_op jit(solution)/shard_map/all_gather | solution.py:36
  176.8 3.2 fusion.2
  179.9 30.8 %all-to-all-done.1 = f32[128,64,128]{2,1,0:T(8,128)} async-done(((f32[128,64,128]{2,1,0:T(8,128)}), f32[128,64,128]{2,1,0:T(8,128)}, u32[]{:S(2)}, u32[]{:S(2)}) %all-to-all-start.1) | async-done | bytes 4194336 | tf_op jit(solution)/shard_map/all_to_all | solution.py:12
  210.8 4.0 gather_fusion.4
  214.8 4.9 fusion.15
  223.7 6.9 %scatter_fusion.1 = f32[128,64,128]{2,1,0:T(8,128)} fusion(f32[128,64,128]{2,1,0:T(8,128)} %broadcast.140, s32[48]{0:T(128)S(1)} %pad_add_fusion, f32[48,64,128]{2,1,0:T(8,128)S(1)} %pad_maximum_fusion), kind=kCustom, calls=%fused_computation.7 | custom fusion | flops 393216 | bytes 4718784 | tf_op jit(solution)/shard_map/scatter-add | solution.py:91
  235.1 2.7 gather_fusion.2
  238.3 72.6 %reduce-scatter.5.cloned.1.call-done = f32[4,64,128]{2,1,0:T(8,128)} async-done(((f32[128,64,128]{2,1,0:T(8,128)}), f32[4,64,128]{2,1,0:T(8,128)}) %reduce-scatter.5.cloned.1.call-update) | async-done | bytes 131088 | tf_op jit(solution)/shard_map/reduce_scatter | solution.py:92
  312.9 146.4 %all-reduce.2.cloned.1.call-done = f32[4,64,64]{2,1,0:T(8,128)} async-done(((f32[4,64,64]{2,1,0:T(8,128)}), f32[4,64,64]{2,1,0:T(8,128)}) %all-reduce.2.cloned.1.call-update) | async-done | bytes 65552 | tf_op jit(solution)/shard_map/psum | solution.py:97
  461.3 5.9 %cholesky.59 = f32[64,64]{1,0:T(8,128)S(1)} custom-call(f32[64,64]{1,0:T(8,128)S(1)} %copy.82), custom_call_target="Cholesky" | custom-call | tf_op jit(solution)/shard_map/jit(cholesky)/cholesky | solution.py:16
  468.5 4.9 custom-call.13
  474.4 5.9 %cholesky.70 = f32[64,64]{1,0:T(8,128)S(1)} custom-call(f32[64,64]{1,0:T(8,128)S(1)} %copy.85), custom_call_target="Cholesky" | custom-call | tf_op jit(solution)/shard_map/jit(cholesky)/cholesky | solution.py:16
  481.7 4.9 custom-call.15
  491.6 5.8 %cholesky.81 = f32[64,64]{1,0:T(8,128)S(1)} custom-call(f32[64,64]{1,0:T(8,128)S(1)} %fusion.51), custom_call_target="Cholesky" | custom-call | tf_op jit(solution)/shard_map/jit(cholesky)/cholesky | solution.py:16
  498.8 4.9 custom-call.17
  (180 shorter events, 82.3 us)
Async XLA Ops:
  7.2 113.2 %copy-start = (f32[2,4,128,128]{3,2,1,0:T(8,128)S(1)}, f32[2,4,128,128]{3,2,1,0:T(8,128)}, u32[]{:S(2)}) copy-start(f32[2,4,128,128]{3,2,1,0:T(8,128)} %param.19) | copy-start | bytes 1572868
  7.2 123.5 %reduce-scatter.3.cloned.1.call-start = ((), (), s32[]{:S(2)}) async-start(), calls=%async_computation.4 | async-start | bytes 4325376 | tf_op jit(solution)/shard_map/reduce_scatter | solution.py:88
  15.4 6.9 %copy-start.1 = (f32[4,64,128]{2,1,0:T(8,128)S(1)}, f32[4,64,128]{2,1,0:T(8,128)}, u32[]{:S(2)}) copy-start(f32[4,64,128]{2,1,0:T(8,128)} %param.16) | copy-start | bytes 393220
  43.3 10.5 %slice-start = ((f32[4,64,128]{2,1,0:T(8,128)}), f32[2,64,128]{2,1,0:T(8,128)S(1)}, s32[]{:S(2)}) async-start(f32[4,64,128]{2,1,0:T(8,128)} %param.16), calls=%async_computation.7 | async-start | bytes 131072 | tf_op jit(solution)/shard_map/slice | solution.py:36
  43.3 67.0 %all-to-all-start = ((f32[128,64,128]{2,1,0:T(8,128)}), f32[128,64,128]{2,1,0:T(8,128)}, u32[]{:S(2)}, u32[]{:S(2)}) async-start(f32[128,64,128]{2,1,0:T(8,128)} %constant_dynamic-update-slice_fusion), calls=%async_computation | async-start | bytes 8388608 | tf_op jit(solution)/shard_map/all_to_all | solution.py:12
  65.2 49.1 %copy-start.2 = (f32[4,11,128,128]{3,2,1,0:T(8,128)S(1)}, f32[4,11,128,128]{3,2,1,0:T(8,128)}, u32[]{:S(2)}) copy-start(f32[4,11,128,128]{3,2,1,0:T(8,128)} %param.18) | copy-start | bytes 8650756
  114.2 4.9 copy-start.6
  114.2 6.1 %copy-start.5 = (f32[8,64,128]{2,1,0:T(8,128)S(1)}, f32[8,64,128]{2,1,0:T(8,128)}, u32[]{:S(2)}) copy-start(f32[8,64,128]{2,1,0:T(8,128)} %all_gather.6) | copy-start | bytes 786436
  152.7 58.1 %all-to-all-start.1 = ((f32[128,64,128]{2,1,0:T(8,128)}), f32[128,64,128]{2,1,0:T(8,128)}, u32[]{:S(2)}, u32[]{:S(2)}) async-start(f32[128,64,128]{2,1,0:T(8,128)} %constant_dynamic-update-slice_fusion.32), calls=%async_computation.2 | async-start | bytes 8388608 | tf_op jit(solution)/shard_map/all_to_all | solution.py:12
  160.1 150.9 %reduce-scatter.5.cloned.1.call-start = ((), (), s32[]{:S(2)}) async-start(), calls=%async_computation.5 | async-start | bytes 4325376 | tf_op jit(solution)/shard_map/reduce_scatter | solution.py:92
  214.8 4.9 copy-start.7
  214.8 5.6 %copy-start.4 = (f32[8,64,128]{2,1,0:T(8,128)S(1)}, f32[8,64,128]{2,1,0:T(8,128)}, u32[]{:S(2)}) copy-start(f32[8,64,128]{2,1,0:T(8,128)} %all_gather.7) | copy-start | bytes 786436
  214.8 6.2 %copy-start.3 = (f32[4,11,128,64]{2,3,1,0:T(8,128)S(1)}, f32[4,11,128,64]{2,3,1,0:T(8,128)}, u32[]{:S(2)}) copy-start(f32[4,11,128,64]{2,3,1,0:T(8,128)} %fusion.2) | copy-start | bytes 4325380
  230.6 228.7 %all-reduce.2.cloned.1.call-start = ((), (), s32[]{:S(2)}) async-start(), calls=%async_computation.6 | async-start | bytes 262144 | tf_op jit(solution)/shard_map/psum | solution.py:97
  311.0 193.7 %copy-start.8 = (f32[4,64,128]{2,1,0:T(8,128)S(1)}, f32[4,64,128]{2,1,0:T(8,128)}, u32[]{:S(2)}) copy-start(f32[4,64,128]{2,1,0:T(8,128)} %reduce-scatter.5.cloned.1.call-done) | copy-start | bytes 393220
Sparse Core Ops, SparseCore 0:
  22.4 108.2 reduce-scatter.2
  230.7 80.2 reduce-scatter.4
  316.3 142.9 all-reduce.1
